TPU v7x, 512 devices: a whole 4x4x16 slice. The times are simulated.
512 devices in a mesh: dp: 32 (over z_lo, y), mp: 16 (over z_hi, x, core).
Axes of the slice: x: 4, y: 4, z: 16 (z_hi: 2, z_lo: 8; z = z_hi * 8 + z_lo), core: 2. Of those that a mesh axis runs over, the one named last changes fastest.
Arguments:
- hidden_in: bfloat16 [12288, 2048], P(('dp', 'mp')), may hold values from -12 to 12
- segment_ids: int32 [32, 384], P('dp'), may hold values from 0 to 7, never falling along the last dimension, each value on 1 to 192 neighbouring positions
- page_table: int32 [32, 3], P('dp'), may hold values from 0 to 2, each once within a row
- qkv_master: float32 [2048, 6144], P(('dp', 'mp')), may hold values from -0.3 to 0.3
- up_master: float32 [2048, 8192], P(('dp', 'mp')), may hold values from -0.125 to 0.125
- dense_weight: bfloat16 [2048, 2048], P('mp'), may hold values from -0.125 to 0.125
Outputs:
- hidden_out: bfloat16 [12288, 2048], P(('dp', 'mp'))
- activated: bfloat16 [12288, 8192], P('dp', 'mp')
- cache_pages: bfloat16 [96, 2, 16, 128, 128], P('dp', None, 'mp')
Inputs may be any that keep to these rules, and one draw needn't show every extreme that they name: `segment_ids`: within a group segment ids never fall; each request holds 1 to 192 tokens and one holds exactly that many. `page_table`: each row names every slot of its group once.
All inputs are finite; a program needn't handle non-finite values.
Results may differ from a plain program's by a relative error of at most 0.015.
Values may be sent and summed in bfloat16 or wider, within the bound.
A program may use at most 64 MiB of HBM per device.

v0:
```python
import jax
import jax.numpy as jnp
from jax import lax
from jax.sharding import PartitionSpec as P

H = 16
HD = 128
PAGE = 128


def layer_norm(values):
    mean_val = jnp.mean(values, -1, keepdims=True)
    centered = values - mean_val
    variance = jnp.mean(centered * centered, -1, keepdims=True)
    return centered * lax.rsqrt(variance + 1e-05)


def reorder_rows(weights, mp_count, dp_count):
    block = weights.shape[0] // (mp_count * dp_count)
    shaped = weights.reshape(mp_count, dp_count, block, weights.shape[1])
    return shaped.transpose(1, 0, 2, 3).reshape(weights.shape[0], weights.shape[1])


def attend(normed, qkv_w, segment, table, mp_index):
    group_rows = normed.shape[0]
    heads_dev = qkv_w.shape[1] // (3 * HD)
    joined = jnp.dot(normed, qkv_w, preferred_element_type=jnp.float32).astype(jnp.bfloat16)
    joined = joined.reshape(group_rows, heads_dev, 3, HD)
    query = joined[:, :, 0]
    keys = joined[:, :, 1]
    vals = joined[:, :, 2]
    head_ids = mp_index * heads_dev + jnp.arange(heads_dev)
    slopes = jnp.exp2(-8.0 * (head_ids + 1).astype(jnp.float32) / H)
    positions = jnp.arange(group_rows)
    distance = (positions[:, None] - positions[None, :]).astype(jnp.float32)
    allowed = (segment[:, None] == segment[None, :]) & (distance >= 0)
    scores = jnp.einsum("thd,shd->hts", query, keys, preferred_element_type=jnp.float32) / jnp.sqrt(
        jnp.float32(HD)
    )
    scores = scores - slopes[:, None, None] * distance[None]
    scores = jnp.where(allowed[None], scores, -jnp.inf)
    probs = jax.nn.softmax(scores, axis=-1).astype(jnp.bfloat16)
    context = jnp.einsum("hts,shd->thd", probs, vals, preferred_element_type=jnp.float32).astype(
        jnp.bfloat16
    )
    context = context.reshape(group_rows, heads_dev * HD)
    key_vals = jnp.stack([keys, vals], 1)
    pages_here = group_rows // PAGE
    key_vals = key_vals.reshape(pages_here, PAGE, 2, heads_dev, HD).transpose(0, 2, 3, 1, 4)
    cache = jnp.zeros((pages_here, 2, heads_dev, PAGE, HD), jnp.bfloat16).at[table].set(key_vals)
    return (context, cache)


def local(hidden_in, segment_ids, page_table, qkv_master, up_master, dense_weight):
    mp_count = lax.axis_size("mp")
    dp_count = lax.axis_size("dp")
    mp_index = lax.axis_index("mp")
    qkv_bf = qkv_master.astype(jnp.bfloat16)
    up_bf = up_master.astype(jnp.bfloat16)
    qkv_rows, up_rows = (
        lax.all_gather(qkv_bf, "dp", axis=0, tiled=True),
        lax.all_gather(up_bf, "dp", axis=0, tiled=True),
    )
    qkv_cols, up_cols = (
        lax.all_to_all(qkv_rows, "mp", split_axis=1, concat_axis=0, tiled=True),
        lax.all_to_all(up_rows, "mp", split_axis=1, concat_axis=0, tiled=True),
    )
    qkv_w = reorder_rows(qkv_cols, mp_count, dp_count)
    up_w = reorder_rows(up_cols, mp_count, dp_count)
    normed_own = layer_norm(hidden_in.astype(jnp.float32)).astype(jnp.bfloat16)
    normed = lax.all_gather(normed_own, "mp", axis=0, tiled=True)
    context, cache = attend(normed, qkv_w, segment_ids[0], page_table[0], mp_index)
    share = lax.psum_scatter(
        jnp.dot(context, dense_weight, preferred_element_type=jnp.float32).astype(jnp.bfloat16),
        "mp",
        scatter_dimension=0,
        tiled=True,
    ).astype(jnp.float32)
    stream_own = hidden_in.astype(jnp.float32) + share
    normed_two = lax.all_gather(
        layer_norm(stream_own).astype(jnp.bfloat16), "mp", axis=0, tiled=True
    )
    upper = jnp.dot(normed_two, up_w, preferred_element_type=jnp.float32)
    activated = jax.nn.gelu(upper, approximate=True).astype(jnp.bfloat16)
    return (stream_own.astype(jnp.bfloat16), activated, cache)


def solution(mesh):
    placed = (
        P(("dp", "mp"), None),
        P("dp", None),
        P("dp", None),
        P(("dp", "mp"), None),
        P(("dp", "mp"), None),
        P("mp", None),
    )
    return jax.shard_map(
        local,
        mesh=mesh,
        in_specs=placed,
        out_specs=(P(("dp", "mp"), None), P("dp", "mp"), P("dp", None, "mp", None, None)),
        check_vma=False,
    )
```

profile of v0, /device:TPU:1, one launch (start us, length us, event | category | flops | bytes accessed | tf_op | source)
XLA Modules:
  0.0 827.7 jit_solution(535030976519693917)
XLA Ops:
  7.2 0.0 copy-start
  7.2 0.0 all-gather.11.cloned.1.call-start
  7.2 1.6 convert_bitcast_fusion.1
  8.8 0.0 all-gather.11.cloned.1.call-update
  8.8 0.0 all-gather.13.cloned.1.call-start
  8.9 1.6 convert_bitcast_fusion
  10.4 0.0 all-gather.13.cloned.1.call-update
  10.5 207.6 %all-gather.11.cloned.1.call-done = bf16[32,4,6144]{2,1,0:T(4,128)(2,1)} async-done(((bf16[1,4,6144]{2,1,0:T(4,128)(2,1)}), bf16[32,4,6144]{2,1,0:T(4,128)(2,1)}) %all-gather.11.cloned.1.call-update) | async-done | bytes 1572880 | tf_op jit(solution)/shard_map/all_gather | solution.py:61
  218.1 3.1 all_to_all.24
  221.1 1.6 copy.20
  222.7 0.0 copy-start.1
  222.7 54.5 %all-to-all-start = ((bf16[128,16,384]{2,0,1:T(8,128)(2,1)}), bf16[128,16,384]{2,0,1:T(8,128)(2,1)}, u32[]{:S(2)}, u32[]{:S(2)}) async-start(bf16[128,16,384]{2,0,1:T(8,128)(2,1)} %copy.20), calls=%async_computation | async-start | bytes 3145728 | tf_op jit(solution)/shard_map/all_to_all | solution.py:65
  277.2 0.0 all-gather.7.cloned.1.call-start
  277.3 0.0 copy-done.1
  277.3 0.1 convert_reduce_fusion
  277.4 0.2 fusion.19
  277.7 0.7 fusion.20
  278.4 0.0 all-gather.7.cloned.1.call-update
  278.4 184.5 %all-gather.13.cloned.1.call-done = bf16[32,4,8192]{2,1,0:T(4,128)(2,1)} async-done(((bf16[1,4,8192]{2,1,0:T(4,128)(2,1)}), bf16[32,4,8192]{2,1,0:T(4,128)(2,1)}) %all-gather.13.cloned.1.call-update) | async-done | bytes 2097168 | tf_op jit(solution)/shard_map/all_gather | solution.py:62
  463.0 3.3 all_to_all.27
  466.2 2.5 copy.25
  468.7 0.0 copy-start.5
  468.7 0.0 all-to-all-done
  468.7 54.6 %all-to-all-start.1 = ((bf16[128,16,512]{2,0,1:T(8,128)(2,1)}), bf16[128,16,512]{2,0,1:T(8,128)(2,1)S(1)}, u32[]{:S(2)}, u32[]{:S(2)}) async-start(bf16[128,16,512]{2,0,1:T(8,128)(2,1)} %copy.25), calls=%async_computation.2 | async-start | bytes 4194304 | tf_op jit(solution)/shard_map/all_to_all | solution.py:66
  523.4 0.0 reduce-scatter.2.cloned.1.call-start
  523.5 0.0 copy-done.5
  523.5 2.3 copy.21
  525.8 2.0 copy.22
  527.8 3.7 reshape.134
  531.6 93.0 %all-gather.7.cloned.1.call-done = bf16[384,2048]{1,0:T(8,128)(2,1)} async-done(((bf16[24,2048]{1,0:T(8,128)(2,1)}), bf16[384,2048]{1,0:T(8,128)(2,1)}) %all-gather.7.cloned.1.call-update) | async-done | bytes 1572880 | tf_op jit(solution)/shard_map/all_gather | solution.py:71
  624.6 2.9 convolution_convert_fusion.1
  627.5 0.0 copy-start.3
  627.5 0.7 copy-done.3
  628.2 0.4 fusion.31
  628.6 0.1 fusion.12
  628.8 0.0 copy-done
  628.8 2.8 convolution_convert_fusion
  631.6 0.0 copy-start.6
  631.6 0.0 copy-start.4
  631.6 0.0 reduce-scatter.2.cloned.1.call-update
  631.6 0.2 all-gather.9.cloned.1.call-start
  631.9 103.5 %reduce-scatter.2.cloned.1.call-done = bf16[24,2048]{1,0:T(8,128)(2,1)} async-done(((bf16[384,2048]{1,0:T(8,128)(2,1)}), bf16[24,2048]{1,0:T(8,128)(2,1)}) %reduce-scatter.2.cloned.1.call-update) | async-done | bytes 98320 | tf_op jit(solution)/shard_map/reduce_scatter | solution.py:73
  735.4 1.0 fusion.21
  736.4 1.1 multiply_reduce_fusion
  737.5 1.6 multiply_convert_fusion
  739.1 0.0 all-gather.9.cloned.1.call-update
  739.2 0.0 copy-done.6
  739.2 0.0 copy-done.4
  739.2 0.1 copy.31
  739.3 0.1 copy.30
  739.6 0.8 scatter_fusion
  740.4 0.0 copy-start.2
  740.4 0.0 all-to-all-done.1
  740.4 1.2 copy.26
  741.6 0.0 copy-done.2
  741.6 2.0 copy.27
  743.6 2.1 reshape.141
  745.6 71.5 %all-gather.9.cloned.1.call-done = bf16[384,2048]{1,0:T(8,128)(2,1)} async-done(((bf16[24,2048]{1,0:T(8,128)(2,1)}), bf16[384,2048]{1,0:T(8,128)(2,1)}) %all-gather.9.cloned.1.call-update) | async-done | bytes 1572880 | tf_op jit(solution)/shard_map/all_gather | solution.py:80
  817.2 3.9 fusion.10
  (10 shorter events, 0.1 us)
Async XLA Ops:
  7.2 621.6 %copy-start = (bf16[128,2048]{1,0:T(8,128)(2,1)S(1)}, bf16[128,2048]{1,0:T(8,128)(2,1)}, u32[]{:S(2)}) copy-start(bf16[128,2048]{1,0:T(8,128)(2,1)} %param.11) | copy-start | bytes 1572868
  7.2 210.9 %all-gather.11.cloned.1.call-start = ((), (), s32[]{:S(2)}) async-start(), calls=%async_computation.6 | async-start | bytes 1622016 | tf_op jit(solution)/shard_map/all_gather | solution.py:61
  8.8 454.1 %all-gather.13.cloned.1.call-start = ((), (), s32[]{:S(2)}) async-start(), calls=%async_computation.7 | async-start | bytes 2162688 | tf_op jit(solution)/shard_map/all_gather | solution.py:62
  222.7 54.6 %copy-start.1 = (bf16[24,2048]{1,0:T(8,128)(2,1)S(1)}, bf16[24,2048]{1,0:T(8,128)(2,1)}, u32[]{:S(2)}) copy-start(bf16[24,2048]{1,0:T(8,128)(2,1)} %param.6) | copy-start | bytes 294916
  222.7 246.0 %all-to-all-start = ((bf16[128,16,384]{2,0,1:T(8,128)(2,1)}), bf16[128,16,384]{2,0,1:T(8,128)(2,1)}, u32[]{:S(2)}, u32[]{:S(2)}) async-start(bf16[128,16,384]{2,0,1:T(8,128)(2,1)} %copy.20), calls=%async_computation | async-start | bytes 3145728 | tf_op jit(solution)/shard_map/all_to_all | solution.py:65
  277.2 347.4 %all-gather.7.cloned.1.call-start = ((), (), s32[]{:S(2)}) async-start(), calls=%async_computation.3 | async-start | bytes 1671168 | tf_op jit(solution)/shard_map/all_gather | solution.py:71
  468.7 54.7 %copy-start.5 = (s32[1,384]{1,0:T(1,128)S(1)}, s32[1,384]{1,0:T(1,128)}, u32[]{:S(2)}) copy-start(s32[1,384]{1,0:T(1,128)} %param.7) | copy-start | bytes 4612
  468.7 271.7 %all-to-all-start.1 = ((bf16[128,16,512]{2,0,1:T(8,128)(2,1)}), bf16[128,16,512]{2,0,1:T(8,128)(2,1)S(1)}, u32[]{:S(2)}, u32[]{:S(2)}) async-start(bf16[128,16,512]{2,0,1:T(8,128)(2,1)} %copy.25), calls=%async_computation.2 | async-start | bytes 4194304 | tf_op jit(solution)/shard_map/all_to_all | solution.py:66
  523.4 212.0 %reduce-scatter.2.cloned.1.call-start = ((), (), s32[]{:S(2)}) async-start(), calls=%async_computation.4 | async-start | bytes 1671168 | tf_op jit(solution)/shard_map/reduce_scatter | solution.py:73
  627.5 0.7 copy-start.3
  631.6 107.5 %copy-start.6 = (s32[1,3]{1,0:T(1,128)S(1)}, s32[1,3]{1,0:T(1,128)}, u32[]{:S(2)}) copy-start(s32[1,3]{1,0:T(1,128)} %param.8) | copy-start | bytes 40
  631.6 107.6 %copy-start.4 = (bf16[384,384]{0,1:T(8,128)(2,1)S(1)}, bf16[384,384]{0,1:T(8,128)(2,1)}, u32[]{:S(2)}) copy-start(bf16[384,384]{0,1:T(8,128)(2,1)} %copy-done.3) | copy-start | bytes 884740
  631.6 185.6 %all-gather.9.cloned.1.call-start = ((), (), s32[]{:S(2)}) async-start(), calls=%async_computation.5 | async-start | bytes 1671168 | tf_op jit(solution)/shard_map/all_gather | solution.py:80
  740.4 1.2 copy-start.2
Sparse Core Ops, SparseCore 0:
  10.7 207.3 all-gather.10
  220.7 242.2 all-gather.12
  466.9 157.6 all-gather.6
  631.8 103.5 reduce-scatter.1
  739.3 77.8 all-gather.8
where the time goes:
time: 828 us
  waiting for transfers between devices  660 us (80%)
  starting transfers between devices  110 us (13%)
  local copies, waits for them, and re-layouts  25.5 us (3%)
  between operations  14 us (2%)
  matrix products  10.1 us (1%)
    all_gather x1, waiting for transfers between devices, local(): lax.all_gather(qkv_bf, 'dp', axis=0, tiled=True)  208 us
    all_gather x1, waiting for transfers between devices, local(): lax.all_gather(up_bf, 'dp', axis=0, tiled=True)  185 us
    reduce_scatter x1, waiting for transfers between devices, local(): lax.psum_scatter(jnp.dot(context, dense_weight, preferred_element_type=jn...  104 us
    all_gather x1, waiting for transfers between devices, local(): normed = lax.all_gather(normed_own, 'mp', axis=0, tiled=True)  93 us
    all_gather x1, waiting for transfers between devices, local(): lax.all_gather(layer_norm(stream_own).astype(jnp.bfloat16), 'mp', axis=0,...  71.5 us
    all_to_all x1, starting transfers between devices, local(): lax.all_to_all(up_rows, 'mp', split_axis=1, concat_axis=0, tiled=True)  54.6 us
    all_to_all x1, starting transfers between devices, local(): lax.all_to_all(qkv_rows, 'mp', split_axis=1, concat_axis=0, tiled=True)  54.5 us
  transfers between devices with their start and end apart: 7, of which 5 were waited for; matrix products, arithmetic and copies ran while one was open for 4% of the time, Pallas kernels for 0%

commit v1 on v0

--- a/solution.py
+++ b/solution.py
@@ -58,7 +58,9 @@
     qkv_bf = qkv_master.astype(jnp.bfloat16)
     up_bf = up_master.astype(jnp.bfloat16)
     qkv_rows, up_rows = (
-        lax.all_gather(qkv_bf, "dp", axis=0, tiled=True),
+        jnp.concatenate(
+            lax.all_to_all(jnp.stack([qkv_bf] * lax.axis_size("dp")), "dp", 0, 0), axis=0
+        ),
         lax.all_gather(up_bf, "dp", axis=0, tiled=True),
     )
     qkv_cols, up_cols = (

time: 828 us -> 638 us (0.77)
  waiting for transfers between devices: 660 us -> 484 us
  starting transfers between devices: 110 us -> 95.6 us
    all_gather x1 -> x0, waiting for transfers between devices: 208 us -> none  [local(): lax.all_gather(qkv_bf, 'dp', axis=0, tiled=True)]
    all_to_all x0 -> x1, waiting for transfers between devices: none -> 78.3 us  [local(): lax.all_to_all(jnp.stack([qkv_bf] * lax.axis_size('dp')), 'dp', 0, 0)]
    all_to_all x1, starting transfers between devices: 54.5 us -> 12.5 us  [local(): lax.all_to_all(qkv_rows, 'mp', split_axis=1, concat_axis=0, tiled=True)]
    all_gather x1, waiting for transfers between devices: 185 us -> 147 us  [local(): lax.all_gather(up_bf, 'dp', axis=0, tiled=True)]
    all_to_all x0 -> x1, starting transfers between devices: none -> 16.2 us  [local(): lax.all_to_all(jnp.stack([qkv_bf] * lax.axis_size('dp')), 'dp', 0, 0)]
    all_to_all x1, starting transfers between devices: 54.6 us -> 66.6 us  [local(): lax.all_to_all(up_rows, 'mp', split_axis=1, concat_axis=0, tiled=True)]
    all_gather x1, waiting for transfers between devices: 93 us -> 83.9 us  [local(): normed = lax.all_gather(normed_own, 'mp', axis=0, tiled=True)]
  transfers between devices with their start and end apart: 7 -> 7, of which waited for: 5 -> 5; matrix products, arithmetic and copies ran while one was open for 4% -> 5% of each run, Pallas kernels for 0% -> 0%
where the time goes in v1:
time: 638 us; the launch traced here: 637 us
  waiting for transfers between devices  484 us (76%)
  starting transfers between devices  95.6 us (15%)
  local copies, waits for them, and re-layouts  27.6 us (4%)
  between operations  14 us (2%)
  matrix products  9.42 us (1%)
  other arithmetic  6.65 us (1%)
    all_gather x1, waiting for transfers between devices, local(): lax.all_gather(up_bf, 'dp', axis=0, tiled=True)  147 us
    reduce_scatter x1, waiting for transfers between devices, local(): lax.psum_scatter(jnp.dot(context, dense_weight, preferred_element_type=jn...  103 us
    all_gather x1, waiting for transfers between devices, local(): normed = lax.all_gather(normed_own, 'mp', axis=0, tiled=True)  83.9 us
    all_to_all x1, waiting for transfers between devices, local(): lax.all_to_all(jnp.stack([qkv_bf] * lax.axis_size('dp')), 'dp', 0, 0)  78.3 us
    all_gather x1, waiting for transfers between devices, local(): lax.all_gather(layer_norm(stream_own).astype(jnp.bfloat16), 'mp', axis=0,...  71.6 us
    all_to_all x1, starting transfers between devices, local(): lax.all_to_all(up_rows, 'mp', split_axis=1, concat_axis=0, tiled=True)  66.6 us
    all_to_all x1, starting transfers between devices, local(): lax.all_to_all(jnp.stack([qkv_bf] * lax.axis_size('dp')), 'dp', 0, 0)  16.2 us
  transfers between devices with their start and end apart: 7, of which 5 were waited for; matrix products, arithmetic and copies ran while one was open for 5% of the time, Pallas kernels for 0%

profile of v1, /device:TPU:1, one launch (start us, length us, event | category | flops | bytes accessed | tf_op | source)
XLA Modules:
  0.0 637.2 jit_solution(4843343853089383723)
XLA Ops:
  7.2 0.0 copy-start
  7.2 1.0 convert_element_type.55
  8.2 1.9 stack.4
  10.0 0.0 copy-start.6
  10.0 16.2 %all-to-all-start = ((bf16[32,4,6144]{2,1,0:T(4,128)(2,1)}), bf16[32,4,6144]{2,1,0:T(4,128)(2,1)S(1)}, u32[]{:S(2)}, u32[]{:S(2)}) async-start(bf16[32,4,6144]{2,1,0:T(4,128)(2,1)} %stack.4), calls=%async_computation | async-start | bytes 3145728 | tf_op jit(solution)/shard_map/all_to_all | solution.py:62
  26.2 0.0 all-gather.9.cloned.1.call-start
  26.3 0.0 copy-done.6
  26.3 0.7 convert_bitcast_fusion
  27.0 0.0 all-gather.9.cloned.1.call-update
  27.0 78.3 %all-to-all-done = bf16[32,4,6144]{2,1,0:T(4,128)(2,1)S(1)} async-done(((bf16[32,4,6144]{2,1,0:T(4,128)(2,1)}), bf16[32,4,6144]{2,1,0:T(4,128)(2,1)S(1)}, u32[]{:S(2)}, u32[]{:S(2)}) %all-to-all-start) | async-done | bytes 1572896 | tf_op jit(solution)/shard_map/all_to_all | solution.py:62
  105.3 1.9 all_to_all.28
  107.2 2.9 copy.29
  110.1 0.0 copy-start.1
  110.1 12.5 %all-to-all-start.1 = ((bf16[128,16,384]{2,0,1:T(8,128)(2,1)}), bf16[128,16,384]{2,0,1:T(8,128)(2,1)}, u32[]{:S(2)}, u32[]{:S(2)}) async-start(bf16[128,16,384]{2,0,1:T(8,128)(2,1)} %copy.29), calls=%async_computation.1 | async-start | bytes 3145728 | tf_op jit(solution)/shard_map/all_to_all | solution.py:67
  122.6 0.0 all-gather.5.cloned.1.call-start
  122.6 0.0 copy-done.1
  122.6 0.1 convert_reduce_fusion
  122.8 0.2 fusion.19
  123.0 0.7 fusion.20
  123.7 0.0 all-gather.5.cloned.1.call-update
  123.8 146.6 %all-gather.9.cloned.1.call-done = bf16[32,4,8192]{2,1,0:T(4,128)(2,1)} async-done(((bf16[1,4,8192]{2,1,0:T(4,128)(2,1)}), bf16[32,4,8192]{2,1,0:T(4,128)(2,1)}) %all-gather.9.cloned.1.call-update) | async-done | bytes 2097168 | tf_op jit(solution)/shard_map/all_gather | solution.py:64
  270.3 3.3 all_to_all.31
  273.6 2.5 copy.34
  276.1 0.0 copy-start.7
  276.1 0.0 all-to-all-done.1
  276.1 66.6 %all-to-all-start.2 = ((bf16[128,16,512]{2,0,1:T(8,128)(2,1)}), bf16[128,16,512]{2,0,1:T(8,128)(2,1)S(1)}, u32[]{:S(2)}, u32[]{:S(2)}) async-start(bf16[128,16,512]{2,0,1:T(8,128)(2,1)} %copy.34), calls=%async_computation.3 | async-start | bytes 4194304 | tf_op jit(solution)/shard_map/all_to_all | solution.py:68
  342.7 0.0 reduce-scatter.2.cloned.1.call-start
  342.8 0.0 copy-done.7
  342.8 2.3 copy.30
  345.1 2.0 copy.31
  347.1 3.7 reshape.138
  350.9 83.9 %all-gather.5.cloned.1.call-done = bf16[384,2048]{1,0:T(8,128)(2,1)} async-done(((bf16[24,2048]{1,0:T(8,128)(2,1)}), bf16[384,2048]{1,0:T(8,128)(2,1)}) %all-gather.5.cloned.1.call-update) | async-done | bytes 1572880 | tf_op jit(solution)/shard_map/all_gather | solution.py:73
  434.8 2.9 convolution_convert_fusion.1
  437.7 0.0 copy-start.4
  437.7 0.7 copy-done.4
  438.4 0.4 fusion.31
  438.8 0.1 fusion.12
  438.9 0.0 copy-done
  438.9 2.8 convolution_convert_fusion
  441.8 0.0 copy-start.8
  441.8 0.0 reduce-scatter.2.cloned.1.call-update
  441.8 0.2 all-gather.7.cloned.1.call-start
  442.0 103.5 %reduce-scatter.2.cloned.1.call-done = bf16[24,2048]{1,0:T(8,128)(2,1)} async-done(((bf16[384,2048]{1,0:T(8,128)(2,1)}), bf16[24,2048]{1,0:T(8,128)(2,1)}) %reduce-scatter.2.cloned.1.call-update) | async-done | bytes 98320 | tf_op jit(solution)/shard_map/reduce_scatter | solution.py:75
  545.5 1.0 fusion.21
  546.5 1.1 multiply_reduce_fusion
  547.6 1.6 multiply_convert_fusion
  549.3 0.0 all-gather.7.cloned.1.call-update
  549.3 0.0 copy-done.8
  549.3 0.0 all-to-all-done.2
  549.3 1.2 copy.35
  550.5 2.0 copy.36
  552.5 0.0 copy-start.5
  552.5 2.1 reshape.145
  554.6 0.0 copy-done.5
  554.6 0.0 copy-start.2
  554.6 0.1 copy.39
  554.7 0.1 copy.40
  554.9 0.8 scatter_fusion
  555.8 0.0 copy-start.3
  555.8 71.6 %all-gather.7.cloned.1.call-done = bf16[384,2048]{1,0:T(8,128)(2,1)} async-done(((bf16[24,2048]{1,0:T(8,128)(2,1)}), bf16[384,2048]{1,0:T(8,128)(2,1)}) %all-gather.7.cloned.1.call-update) | async-done | bytes 1572880 | tf_op jit(solution)/shard_map/all_gather | solution.py:82
  627.4 0.0 copy-done.2
  627.4 3.3 fusion.10
  630.6 0.0 copy-done.3
  (10 shorter events, 0.1 us)
Async XLA Ops:
  7.2 431.7 %copy-start = (bf16[128,2048]{1,0:T(8,128)(2,1)S(1)}, bf16[128,2048]{1,0:T(8,128)(2,1)}, u32[]{:S(2)}) copy-start(bf16[128,2048]{1,0:T(8,128)(2,1)} %param.11) | copy-start | bytes 1572868
  10.0 16.3 %copy-start.6 = (f32[4,8192]{1,0:T(4,128)S(1)}, f32[4,8192]{1,0:T(4,128)}, u32[]{:S(2)}) copy-start(f32[4,8192]{1,0:T(4,128)} %param.10) | copy-start | bytes 393220
  10.0 95.3 %all-to-all-start = ((bf16[32,4,6144]{2,1,0:T(4,128)(2,1)}), bf16[32,4,6144]{2,1,0:T(4,128)(2,1)S(1)}, u32[]{:S(2)}, u32[]{:S(2)}) async-start(bf16[32,4,6144]{2,1,0:T(4,128)(2,1)} %stack.4), calls=%async_computation | async-start | bytes 3145728 | tf_op jit(solution)/shard_map/all_to_all | solution.py:62
  26.2 244.1 %all-gather.9.cloned.1.call-start = ((), (), s32[]{:S(2)}) async-start(), calls=%async_computation.7 | async-start | bytes 2162688 | tf_op jit(solution)/shard_map/all_gather | solution.py:64
  110.1 12.5 %copy-start.1 = (bf16[24,2048]{1,0:T(8,128)(2,1)S(1)}, bf16[24,2048]{1,0:T(8,128)(2,1)}, u32[]{:S(2)}) copy-start(bf16[24,2048]{1,0:T(8,128)(2,1)} %param.6) | copy-start | bytes 294916
  110.1 166.0 %all-to-all-start.1 = ((bf16[128,16,384]{2,0,1:T(8,128)(2,1)}), bf16[128,16,384]{2,0,1:T(8,128)(2,1)}, u32[]{:S(2)}, u32[]{:S(2)}) async-start(bf16[128,16,384]{2,0,1:T(8,128)(2,1)} %copy.29), calls=%async_computation.1 | async-start | bytes 3145728 | tf_op jit(solution)/shard_map/all_to_all | solution.py:67
  122.6 312.2 %all-gather.5.cloned.1.call-start = ((), (), s32[]{:S(2)}) async-start(), calls=%async_computation.4 | async-start | bytes 1671168 | tf_op jit(solution)/shard_map/all_gather | solution.py:73
  276.1 66.7 %copy-start.7 = (s32[1,384]{1,0:T(1,128)S(1)}, s32[1,384]{1,0:T(1,128)}, u32[]{:S(2)}) copy-start(s32[1,384]{1,0:T(1,128)} %param.7) | copy-start | bytes 4612
  276.1 273.2 %all-to-all-start.2 = ((bf16[128,16,512]{2,0,1:T(8,128)(2,1)}), bf16[128,16,512]{2,0,1:T(8,128)(2,1)S(1)}, u32[]{:S(2)}, u32[]{:S(2)}) async-start(bf16[128,16,512]{2,0,1:T(8,128)(2,1)} %copy.34), calls=%async_computation.3 | async-start | bytes 4194304 | tf_op jit(solution)/shard_map/all_to_all | solution.py:68
  342.7 202.8 %reduce-scatter.2.cloned.1.call-start = ((), (), s32[]{:S(2)}) async-start(), calls=%async_computation.5 | async-start | bytes 1671168 | tf_op jit(solution)/shard_map/reduce_scatter | solution.py:75
  437.7 0.7 copy-start.4
  441.8 107.5 %copy-start.8 = (s32[1,3]{1,0:T(1,128)S(1)}, s32[1,3]{1,0:T(1,128)}, u32[]{:S(2)}) copy-start(s32[1,3]{1,0:T(1,128)} %param.8) | copy-start | bytes 40
  441.8 185.6 %all-gather.7.cloned.1.call-start = ((), (), s32[]{:S(2)}) async-start(), calls=%async_computation.6 | async-start | bytes 1671168 | tf_op jit(solution)/shard_map/all_gather | solution.py:82
  552.5 2.1 copy-start.5
  554.6 72.8 %copy-start.2 = (bf16[2048,512]{1,0:T(8,128)(2,1)S(1)}, bf16[2048,512]{1,0:T(8,128)(2,1)}, u32[]{:S(2)}) copy-start(bf16[2048,512]{1,0:T(8,128)(2,1)} %reshape.145) | copy-start | bytes 6291460
  555.8 74.9 %copy-start.3 = (bf16[3,2,128,128]{3,2,1,0:T(8,128)(2,1)}, bf16[3,2,128,128]{3,2,1,0:T(8,128)(2,1)S(1)}, u32[]{:S(2)}) copy-start(bf16[3,2,128,128]{3,2,1,0:T(8,128)(2,1)S(1)} %scatter_fusion) | copy-start | bytes 589828
Sparse Core Ops, SparseCore 0:
  29.7 240.5 all-gather.8
  274.2 160.4 all-gather.4
  441.9 103.5 reduce-scatter.1
  549.4 77.8 all-gather.6
